TPU v7x, 256 devices: a whole 4x4x8 slice. The times are simulated.
256 devices in a mesh: occ: 8 (over z_hi, core), aux: 32 (over x, z_lo, y).
Axes of the slice: x: 4, y: 4, z: 8 (z_hi: 4, z_lo: 2; z = z_hi * 2 + z_lo), core: 2. Of those that a mesh axis runs over, the one named last changes fastest.
Arguments:
- coeffs: bfloat16 [8, 256, 131072], P('occ', None, 'aux'), may hold values from -0.31445312 to 0.31445312
- occ_energy: bfloat16 [8], P('occ'), may hold values from -1.5 to -0.29882812
- virt_energy: bfloat16 [256], replicated, may hold values from 0.19921875 to 3
- screen: int32 [8, 1024], P('occ', 'aux'), may hold values 0 or 1
- owner: int32 [1024], P('aux'), may hold values from 0 to 127
- positions: float32 [3, 128], replicated, may hold values from -1 to 1
Outputs:
- gamma: bfloat16 [8, 256, 131072], P('occ', None, 'aux')
- virial: float32 [9, 131072], P(None, 'aux')
All inputs are finite; a program needn't handle non-finite values. No bound on the sum of `screen` on one device may be relied on, other than what follows from the above.
Results may differ from a plain program's by a relative error of at most 0.0049.
Values may be sent and summed in bfloat16 or wider, within the bound.
A program may use at most 64 MiB of HBM per device.

v0:
```python
import jax
import jax.numpy as jnp
from jax import lax
from jax.sharding import PartitionSpec as P

ABLK = 128


def body(coeffs, occ_energy, virt_energy, screen, owner, positions):
    occ_dev, virt, aux_dev = coeffs.shape
    column_mask = jnp.repeat(screen[0], ABLK).astype(jnp.bfloat16)
    masked = coeffs * column_mask[None, None, :]
    whole, energies = (
        lax.all_gather(masked, "occ", axis=0, tiled=True),
        lax.all_gather(occ_energy, "occ", axis=0, tiled=True),
    )
    all_rows = whole.reshape(-1, aux_dev)
    local = masked.reshape(-1, aux_dev)
    virt_f = virt_energy.astype(jnp.float32)
    spread_local = (virt_f[None, :] - occ_energy.astype(jnp.float32)[:, None]).reshape(-1)
    spread_all = (virt_f[None, :] - energies.astype(jnp.float32)[:, None]).reshape(-1)
    contract_last = (((1,), (1,)), ((), ()))
    contract_first = (((0,), (0,)), ((), ()))
    summed = lax.psum(
        lax.dot_general(all_rows, local, contract_last, preferred_element_type=jnp.float32), "aux"
    )
    amps = (summed / (spread_all[:, None] + spread_local[None, :])).astype(jnp.bfloat16)
    gamma = lax.dot_general(amps, all_rows, contract_first, preferred_element_type=jnp.float32)
    gamma_out = gamma.astype(jnp.bfloat16)
    partial_weight = jnp.sum(gamma_out.astype(jnp.float32) * local.astype(jnp.float32), axis=0)
    weight = lax.psum(partial_weight, "occ")
    atom_ids = jnp.arange(positions.shape[1], dtype=jnp.int32)
    onehot = (owner[:, None] == atom_ids[None, :]).astype(jnp.float32)
    block_where = jnp.dot(onehot, positions.T, precision=lax.Precision.HIGHEST)
    where = jnp.repeat(block_where.T, ABLK, axis=1)
    virial = (where[:, None, :] * where[None, :, :]).reshape(9, aux_dev) * weight[None, :]
    return (gamma_out.reshape(occ_dev, virt, aux_dev), virial)


def solution(mesh):
    placed = (P("occ", None, "aux"), P("occ"), P(), P("occ", "aux"), P("aux"), P())
    return jax.shard_map(
        body,
        mesh=mesh,
        in_specs=placed,
        out_specs=(P("occ", None, "aux"), P(None, "aux")),
        check_vma=False,
    )
```

profile of v0, /device:TPU:8, one launch (start us, length us, event | category | flops | bytes accessed | tf_op | source)
XLA Modules:
  0.0 545.0 jit_solution(9232543608155774374)
XLA Ops:
  7.2 0.0 copy-start
  7.2 0.0 all-gather.2.cloned.1.call-start
  7.2 0.7 convert_bitcast_fusion
  7.9 0.1 broadcast_bitcast_fusion.1
  8.0 3.1 broadcast_multiply_fusion
  11.0 0.0 copy-start.1
  11.0 0.0 all-gather.2.cloned.1.call-update
  11.0 0.0 all-reduce.3.cloned.1.call-start
  11.1 160.1 %all-gather.2.cloned.1.call-done = bf16[8,256,4096]{2,1,0:T(8,128)(2,1)} async-done(((bf16[1,256,4096]{2,1,0:T(8,128)(2,1)}), bf16[8,256,4096]{2,1,0:T(8,128)(2,1)}) %all-gather.2.cloned.1.call-update) | async-done | bytes 16777232 | tf_op jit(solution)/shard_map/all_gather | solution.py:14
  171.2 0.0 copy-done.1
  171.2 9.6 %fusion = f32[2048,256]{1,0:T(8,128)} fusion(bf16[2048,4096]{1,0:T(8,128)(2,1)} %bitcast.29, bf16[1,256,4096]{2,1,0:T(8,128)(2,1)S(1)} %copy-done.1), kind=kOutput, calls=%fused_computation.2 | convolution fusion | flops 4294967296 | bytes 20971520 | tf_op jit(solution)/shard_map/dot_general | solution.py:25
  180.8 0.0 copy-start.4
  180.8 0.0 copy-start.2
  180.8 0.0 copy-start.3
  180.8 0.0 all-reduce.3.cloned.1.call-update
  181.5 0.0 copy-done.4
  181.5 0.6 dynamic-slice
  182.1 0.7 dynamic-update-slice
  182.8 16.4 %all-reduce = bf16[8]{0:T(256)(128)(2,1)S(1)} all-reduce(bf16[8]{0:T(256)(128)(2,1)S(1)} %dynamic-update-slice), channel_id=1, replica_groups=mesh['occ'=8,'aux'=32] {'occ'}, use_global_device_ids=true, to_apply=%add | all-reduce | flops 8 | bytes 32
  199.2 0.0 copy-done.2
  199.2 0.1 subtract_bitcast_fusion
  199.3 0.0 copy-done
  199.3 0.0 copy-done.3
  199.3 0.2 convolution_bitcast_fusion
  199.5 0.1 broadcast_bitcast_fusion
  199.6 0.1 copy.11
  199.7 0.1 mul.44
  199.8 297.7 %all-reduce.3.cloned.1.call-done = f32[2048,256]{1,0:T(8,128)} async-done(((f32[2048,256]{1,0:T(8,128)}), f32[2048,256]{1,0:T(8,128)}) %all-reduce.3.cloned.1.call-update) | async-done | bytes 2097168 | tf_op jit(solution)/shard_map/psum | solution.py:24
  497.5 12.8 %multiply_reduce_fusion = (f32[4096]{0:T(1024)S(1)}, bf16[256,4096]{1,0:T(8,128)(2,1)}) fusion(bf16[1,256,4096]{2,1,0:T(8,128)(2,1)S(1)} %copy-done.1, bf16[2048,4096]{1,0:T(8,128)(2,1)} %bitcast.30, f32[2048,256]{1,0:T(8,128)} %all-reduce.3.cloned.1.call-done, f32[256]{0:T(256)S(1)} %broadcast_subtract_fusion, f32[2048]{0:T(1024)S(1)} %bitcast.28), kind=kOutput, calls=%fused_computation.1 | convolution fusion | flops 4301778944 | bytes 23094272 | tf_op jit(solution)/shard_map/dot_general | solution.py:28
  510.3 27.1 %psum.15 = f32[4096]{0:T(1024)S(1)} all-reduce(f32[4096]{0:T(1024)S(1)} %get-tuple-element.2), channel_id=1, replica_groups=mesh['occ'=8,'aux'=32] {'occ'}, use_global_device_ids=true, to_apply=%region_2.0 | all-reduce | flops 4096 | bytes 32768 | tf_op jit(solution)/shard_map/psum | solution.py:31
  537.4 0.7 broadcast_multiply_fusion.1
  (6 shorter events, 0.1 us)
Async XLA Ops:
  7.2 192.1 %copy-start = (f32[3,128]{1,0:T(4,128)S(1)}, f32[3,128]{1,0:T(4,128)}, u32[]{:S(2)}) copy-start(f32[3,128]{1,0:T(4,128)} %param.11) | copy-start | bytes 4612
  7.2 164.0 %all-gather.2.cloned.1.call-start = ((), (), s32[]{:S(2)}) async-start(), calls=%async_computation | async-start | bytes 18874368 | tf_op jit(solution)/shard_map/all_gather | solution.py:14
  11.0 160.2 %copy-start.1 = (bf16[1,256,4096]{2,1,0:T(8,128)(2,1)S(1)}, bf16[1,256,4096]{2,1,0:T(8,128)(2,1)}, u32[]{:S(2)}) copy-start(bf16[1,256,4096]{2,1,0:T(8,128)(2,1)} %broadcast_multiply_fusion) | copy-start | bytes 6291460
  11.0 486.4 %all-reduce.3.cloned.1.call-start = ((), (), s32[]{:S(2)}) async-start(), calls=%async_computation.1 | async-start | bytes 4194304 | tf_op jit(solution)/shard_map/psum | solution.py:24
  180.8 0.7 copy-start.4
  180.8 18.4 %copy-start.2 = (bf16[256]{0:T(256)(128)(2,1)S(1)}, bf16[256]{0:T(256)(128)(2,1)}, u32[]{:S(2)}) copy-start(bf16[256]{0:T(256)(128)(2,1)} %param.8) | copy-start | bytes 1540
  180.8 18.5 %copy-start.3 = (s32[32]{0:T(128)S(1)}, s32[32]{0:T(128)}, u32[]{:S(2)}) copy-start(s32[32]{0:T(128)} %param.10) | copy-start | bytes 388
Sparse Core Ops, SparseCore 0:
  11.2 159.9 all-gather.1
  181.0 316.4 all-reduce.2
where the time goes:
time: 545 us
  waiting for transfers between devices  458 us (84%)
  blocking collectives  43.5 us (8%)
  matrix products  22.6 us (4%)
  between operations  14.8 us (3%)
    psum x1, waiting for transfers between devices, body(): lax.psum(lax.dot_general(all_rows, local, contract_last, preferred_elemen...  298 us
    all_gather x1, waiting for transfers between devices, body(): lax.all_gather(masked, 'occ', axis=0, tiled=True)  160 us
    psum x1, blocking collectives, body(): weight = lax.psum(partial_weight, 'occ')  27.1 us
    unnamed x1, blocking collectives  16.4 us
    dot_general x1, matrix products, body(): lax.dot_general(amps, all_rows, contract_first, preferred_element_type=jn...  12.8 us
  transfers between devices with their start and end apart: 2, of which 2 were waited for; matrix products, arithmetic and copies ran while one was open for 0% of the time, Pallas kernels for 0%

commit v1 on v0

--- a/solution.py
+++ b/solution.py
@@ -6,12 +6,19 @@
 ABLK = 128
 
 
+def gather_over(x, axis, dim):
+    n_dev = lax.axis_size(axis)
+    blocks = jnp.stack([x for _ in range(n_dev)])
+    blocks = lax.all_to_all(blocks, axis, split_axis=0, concat_axis=0)
+    return jnp.concatenate(blocks, axis=dim)
+
+
 def body(coeffs, occ_energy, virt_energy, screen, owner, positions):
     occ_dev, virt, aux_dev = coeffs.shape
     column_mask = jnp.repeat(screen[0], ABLK).astype(jnp.bfloat16)
     masked = coeffs * column_mask[None, None, :]
     whole, energies = (
-        lax.all_gather(masked, "occ", axis=0, tiled=True),
+        gather_over(masked, "occ", 0),
         lax.all_gather(occ_energy, "occ", axis=0, tiled=True),
     )
     all_rows = whole.reshape(-1, aux_dev)

time: 545 us -> 764 us (1.40)
  blocking collectives: 43.5 us -> 417 us
  waiting for transfers between devices: 458 us -> 299 us
  local copies, waits for them, and re-layouts: 1.64 us -> 9.36 us
    all_to_all x0 -> x1, blocking collectives: none -> 376 us  [gather_over(): blocks = lax.all_to_all(blocks, axis, split_axis=0, concat_axis=0)]
    all_gather x1 -> x0, waiting for transfers between devices: 160 us -> none  [body(): lax.all_gather(masked, 'occ', axis=0, tiled=True)]
  transfers between devices with their start and end apart: 2 -> 1, of which waited for: 2 -> 1; matrix products, arithmetic and copies ran while one was open for 0% -> 0% of each run, Pallas kernels for 0% -> 0%
where the time goes in v1:
time: 764 us; the launch traced here: 763 us
  blocking collectives  417 us (55%)
  waiting for transfers between devices  299 us (39%)
  matrix products  19.4 us (3%)
  between operations  14.8 us (2%)
  local copies, waits for them, and re-layouts  9.36 us (1%)
    all_to_all x1, blocking collectives, gather_over(): blocks = lax.all_to_all(blocks, axis, split_axis=0, concat_axis=0)  376 us
    psum x1, waiting for transfers between devices, body(): lax.psum(lax.dot_general(all_rows, local, contract_last, preferred_elemen...  299 us
    psum x1, blocking collectives, body(): weight = lax.psum(partial_weight, 'occ')  27.1 us
  transfers between devices with their start and end apart: 1, of which 1 were waited for; matrix products, arithmetic and copies ran while one was open for 0% of the time, Pallas kernels for 0%

profile of v1, /device:TPU:8, one launch (start us, length us, event | category | flops | bytes accessed | tf_op | source)
XLA Modules:
  0.0 763.3 jit_solution(15056371594196600784)
XLA Ops:
  7.2 0.0 copy-start
  7.2 0.0 all-reduce.3.cloned.1.call-start
  7.2 0.7 convert_bitcast_fusion
  7.9 0.1 broadcast_bitcast_fusion.1
  8.0 1.7 multiply_bitcast_fusion
  9.7 2.0 stack.2
  11.7 375.7 %all_to_all.5 = bf16[8,1,256,4096]{3,2,1,0:T(8,128)(2,1)S(1)} all-to-all(bf16[8,1,256,4096]{3,2,1,0:T(8,128)(2,1)S(1)} %stack.2), channel_id=1, replica_groups=mesh['occ'=8,'aux'=32] {'occ'}, dimensions={0} | all-to-all | bytes 33554432 | tf_op jit(solution)/shard_map/all_to_all | solution.py:12
  387.4 0.0 copy-start.1
  387.4 5.7 copy-done.1
  393.1 6.4 fusion.3
  399.5 0.0 copy-start.4
  399.5 0.0 copy-start.2
  399.5 0.0 copy-start.3
  399.5 0.0 all-reduce.3.cloned.1.call-update
  400.2 0.0 copy-done.4
  400.2 0.6 dynamic-slice
  400.9 0.7 dynamic-update-slice
  401.6 14.2 %all-reduce = bf16[8]{0:T(256)(128)(2,1)S(1)} all-reduce(bf16[8]{0:T(256)(128)(2,1)S(1)} %dynamic-update-slice), channel_id=1, replica_groups=mesh['occ'=8,'aux'=32] {'occ'}, use_global_device_ids=true, to_apply=%add | all-reduce | flops 8 | bytes 32
  415.8 0.0 copy-done.2
  415.8 0.1 subtract_bitcast_fusion
  415.9 0.0 copy-done
  415.9 0.0 copy-done.3
  415.9 0.2 convolution_bitcast_fusion
  416.1 0.1 broadcast_bitcast_fusion
  416.2 0.1 copy.11
  416.3 0.1 mul.47
  416.4 299.4 %all-reduce.3.cloned.1.call-done = f32[2048,256]{1,0:T(8,128)} async-done(((f32[2048,256]{1,0:T(8,128)}), f32[2048,256]{1,0:T(8,128)}) %all-reduce.3.cloned.1.call-update) | async-done | bytes 2097168 | tf_op jit(solution)/shard_map/psum | solution.py:31
  715.8 12.8 %multiply_reduce_fusion = (f32[4096]{0:T(1024)S(1)}, bf16[256,4096]{1,0:T(8,128)(2,1)}) fusion(bf16[256,4096]{1,0:T(8,128)(2,1)S(1)} %multiply_bitcast_fusion, bf16[2048,4096]{1,0:T(8,128)(2,1)} %bitcast.27, f32[2048,256]{1,0:T(8,128)} %all-reduce.3.cloned.1.call-done, f32[256]{0:T(256)S(1)} %broadcast_subtract_fusion, f32[2048]{0:T(1024)S(1)} %bitcast.29), kind=kOutput, calls=%fused_computation.1 | convolution fusion | flops 4301778944 | bytes 23094272 | tf_op jit(solution)/shard_map/dot_general | solution.py:35
  728.6 27.1 %psum.15 = f32[4096]{0:T(1024)S(1)} all-reduce(f32[4096]{0:T(1024)S(1)} %get-tuple-element.2), channel_id=1, replica_groups=mesh['occ'=8,'aux'=32] {'occ'}, use_global_device_ids=true, to_apply=%region_2.0 | all-reduce | flops 4096 | bytes 32768 | tf_op jit(solution)/shard_map/psum | solution.py:38
  755.7 0.7 broadcast_multiply_fusion
  (6 shorter events, 0.1 us)
Async XLA Ops:
  7.2 408.7 %copy-start = (f32[3,128]{1,0:T(4,128)S(1)}, f32[3,128]{1,0:T(4,128)}, u32[]{:S(2)}) copy-start(f32[3,128]{1,0:T(4,128)} %param.11) | copy-start | bytes 4612
  7.2 708.6 %all-reduce.3.cloned.1.call-start = ((), (), s32[]{:S(2)}) async-start(), calls=%async_computation.1 | async-start | bytes 4194304 | tf_op jit(solution)/shard_map/psum | solution.py:31
  387.4 5.7 copy-start.1
  399.5 0.7 copy-start.4
  399.5 16.3 %copy-start.2 = (bf16[256]{0:T(256)(128)(2,1)S(1)}, bf16[256]{0:T(256)(128)(2,1)}, u32[]{:S(2)}) copy-start(bf16[256]{0:T(256)(128)(2,1)} %param.8) | copy-start | bytes 1540
  399.5 16.4 %copy-start.3 = (s32[32]{0:T(128)S(1)}, s32[32]{0:T(128)}, u32[]{:S(2)}) copy-start(s32[32]{0:T(128)} %param.10) | copy-start | bytes 388
Sparse Core Ops, SparseCore 0:
  399.7 316.0 all-reduce.2
